TPU v7x, 32 devices: a whole 2x2x4 slice. The times are simulated.
32 devices in a mesh: groups: 2 (over y), seq: 4 (over z), head: 2 (over x), sub: 2 (over core).
Axes of the slice: x: 2, y: 2, z: 4, core: 2. Of those that a mesh axis runs over, the one named last changes fastest.
Arguments:
- hidden_states: bfloat16 [8192, 8192], P(('groups', 'seq', 'sub'), 'head'), parts along dimension 0, may hold values from -42 to 42
- key_projection_weight: bfloat16 [8192, 1024], P(('seq', 'sub'), 'head'), may hold values from -0.0625 to 0.0625
- value_projection_weight: bfloat16 [8192, 1024], P(('seq', 'sub'), 'head'), may hold values from -0.0625 to 0.0625
- head_basis_matrix: float32 [8, 128, 64], P('head'), may hold values from -0.5 to 0.5
- slot_token: int32 [8192], P(('groups', 'seq', 'sub')), parts along dimension 0, may hold values from 0 to 4095, as said below
Outputs:
- compressed_keys: bfloat16 [8192, 512], P(('groups', 'seq', 'sub'), 'head'), parts along dimension 0
- value_cache: bfloat16 [8192, 1024], P(('groups', 'seq', 'sub'), 'head'), parts along dimension 0
There are 2 independent parts, one for each index of `groups`. A program takes and returns all parts, laid end to end along the dimension named above; an argument that names none is the same for every part. Nothing has to cross between parts.
Inputs may be any that keep to these rules, and one draw needn't show every extreme that they name: `slot_token`: A permutation of the 4096 token positions. Each aligned block of 512 rows holds exactly 64 positions of each aligned block of 512 positions.
All inputs are finite; a program needn't handle non-finite values.
Results may differ from a plain program's by a relative error of at most 0.0055.
Values may be sent and summed in bfloat16 or wider, within the bound.
No kernel may reach another device: no remote copies, remote signals or barrier semaphores. Data moves between devices by JAX's collectives and lax.ppermute only.
A program may use at most 64 MiB of HBM per device.

v0:
```python
import jax
import jax.numpy as jnp
from jax import lax
from jax.sharding import PartitionSpec as P

ridge_share = 0.05


def covariance_sum(decode_key_cache, heads_here, head_dim, token_total):
    per_head_keys = decode_key_cache.reshape(decode_key_cache.shape[0], heads_here, head_dim)
    local_terms = jnp.einsum(
        "thi,thj->hij", per_head_keys, per_head_keys, preferred_element_type=jnp.float32
    )
    summed = lax.psum(local_terms, ("seq", "sub"))
    return summed / token_total


def per_device(
    hidden_states, key_projection_weight, value_projection_weight, head_basis_matrix, slot_token
):
    tokens_here = hidden_states.shape[0]
    seq_count = lax.axis_size("seq")
    core_count = lax.axis_size("sub")
    device_count = seq_count * core_count
    token_total = tokens_here * device_count
    heads_here = head_basis_matrix.shape[0]
    head_dim = head_basis_matrix.shape[1]
    rank_dim = head_basis_matrix.shape[2]
    gathered = lax.all_gather(hidden_states, "head", axis=1, tiled=True)
    key_sums = jnp.dot(
        gathered,
        lax.all_gather(key_projection_weight, ("seq", "sub"), axis=0, tiled=True),
        preferred_element_type=jnp.float32,
    )
    value_sums = jnp.dot(
        gathered,
        lax.all_gather(value_projection_weight, ("seq", "sub"), axis=0, tiled=True),
        preferred_element_type=jnp.float32,
    )
    decode_key_cache = key_sums.astype(jnp.bfloat16)
    moments = covariance_sum(decode_key_cache, heads_here, head_dim, token_total)
    value_cache = value_sums.astype(jnp.bfloat16)
    trace_vals = jnp.trace(moments, axis1=1, axis2=2)
    identity = jnp.eye(head_dim, dtype=jnp.float32)
    regular = moments + (ridge_share * trace_vals / head_dim)[:, None, None] * identity
    factor = jnp.linalg.cholesky(regular)
    by_head = jnp.transpose(
        decode_key_cache.astype(jnp.float32).reshape(tokens_here, heads_here, head_dim), (1, 0, 2)
    )
    whitened = lax.linalg.triangular_solve(
        factor, by_head, left_side=False, lower=True, transpose_a=True
    )
    basis_coefficients = jnp.einsum(
        "htd,hdr->htr", whitened, head_basis_matrix, precision=lax.Precision.HIGHEST
    )
    compressed = (
        jnp.transpose(basis_coefficients, (1, 0, 2))
        .reshape(tokens_here, heads_here * rank_dim)
        .astype(jnp.bfloat16)
    )
    row_order = jnp.argsort(slot_token)
    wanted = slot_token[row_order]
    asked = lax.all_to_all(wanted, ("seq", "sub"), split_axis=0, concat_axis=0, tiled=True)
    local_rows = asked % tokens_here
    got_coeffs, got_values = (
        lax.all_to_all(
            compressed[local_rows], ("seq", "sub"), split_axis=0, concat_axis=0, tiled=True
        ),
        lax.all_to_all(
            value_cache[local_rows], ("seq", "sub"), split_axis=0, concat_axis=0, tiled=True
        ),
    )
    inverse = jnp.argsort(row_order)
    return (got_coeffs[inverse], got_values[inverse])


def solution(mesh):
    return jax.shard_map(
        per_device,
        mesh=mesh,
        in_specs=(
            P(("groups", "seq", "sub"), "head"),
            P(("seq", "sub"), "head"),
            P(("seq", "sub"), "head"),
            P("head", None, None),
            P(("groups", "seq", "sub")),
        ),
        out_specs=(P(("groups", "seq", "sub"), "head"), P(("groups", "seq", "sub"), "head")),
        check_vma=False,
    )
```

profile of v0, /device:TPU:0, one launch (start us, length us, event | category | flops | bytes accessed | tf_op | source)
XLA Modules:
  0.0 405.3 jit_solution(3034889648175689121)
XLA Ops:
  8.7 107.6 %all-gather.4.cloned.1.call-done = bf16[512,8192]{1,0:T(8,128)(2,1)} async-done(((bf16[512,4096]{1,0:T(8,128)(2,1)}), bf16[512,8192]{1,0:T(8,128)(2,1)}) %all-gather.4.cloned.1.call-update) | async-done | bytes 8388624 | tf_op jit(solution)/shard_map/all_gather | solution.py:29
  116.3 83.7 %all-gather.6.cloned.1.call-done = bf16[8192,512]{1,0:T(8,128)(2,1)} async-done(((bf16[1024,512]{1,0:T(8,128)(2,1)}), bf16[8192,512]{1,0:T(8,128)(2,1)}) %all-gather.6.cloned.1.call-update) | async-done | bytes 8388624 | tf_op jit(solution)/shard_map/all_gather | solution.py:32
  200.0 10.3 %convolution_convert_fusion.1 = bf16[512,512]{0,1:T(8,128)(2,1)S(1)} fusion(bf16[512,8192]{1,0:T(8,128)(2,1)} %all-gather.4.cloned.1.call-done, bf16[8192,512]{1,0:T(8,128)(2,1)} %all-gather.6.cloned.1.call-done), kind=kOutput, calls=%fused_computation.6 | convolution fusion | flops 4295229440 | bytes 17301504 | tf_op jit(solution)/shard_map/dot_general | solution.py:30
  210.3 1.0 fusion.6
  211.9 3.8 sort.31
  215.7 3.5 gather_fusion
  219.9 3.5 all-to-all-start
  223.4 5.2 %all-to-all-done = s32[8,64,1]{1,2,0:T(1,128)S(1)} async-done(((s32[8,64,1]{1,2,0:T(1,128)}), s32[8,64,1]{1,2,0:T(1,128)S(1)}, u32[]{:S(2)}, u32[]{:S(2)}) %all-to-all-start) | async-done | bytes 2080 | tf_op jit(solution)/shard_map/all_to_all | solution.py:63
  230.2 34.9 %all-reduce.2.cloned.1.call-done = f32[4,128,128]{2,1,0:T(8,128)} async-done(((f32[4,128,128]{2,1,0:T(8,128)}), f32[4,128,128]{2,1,0:T(8,128)}) %all-reduce.2.cloned.1.call-update) | async-done | bytes 262160 | tf_op jit(solution)/shard_map/psum | solution.py:14
  265.1 1.1 select_reduce_fusion.1
  266.1 1.0 multiply_add_fusion
  267.3 1.1 fusion.3
  268.4 46.9 %custom-call.7 = f32[4,128,128]{2,1,0:T(8,128)S(1)} custom-call(f32[4,128,128]{2,1,0:T(8,128)S(1)} %fusion.3), custom_call_target="Cholesky" | custom-call | tf_op jit(solution)/shard_map/jit(cholesky)/cholesky | solution.py:46
  315.6 39.3 %custom-call.8 = f32[4,1,128,128]{2,3,1,0:T(8,128)S(1)} custom-call(f32[4,1,128,128]{3,2,1,0:T(8,128)S(1)} %select_bitcast_fusion), custom_call_target="InvertDiagBlocksLowerTriangular" | custom-call | tf_op jit(solution)/shard_map/triangular_solve | solution.py:50
  355.5 1.3 convolution_convert_fusion.2
  356.9 2.6 gather_fusion.1
  359.5 3.6 all-to-all-start.1
  363.1 10.2 %convolution_convert_fusion = bf16[512,512]{1,0:T(8,128)(2,1)S(1)} fusion(bf16[512,8192]{1,0:T(8,128)(2,1)} %all-gather.4.cloned.1.call-done, bf16[8192,512]{1,0:T(8,128)(2,1)} %all-gather.8.cloned.1.call-done), kind=kOutput, calls=%fused_computation.5 | convolution fusion | flops 4295229440 | bytes 17301504 | tf_op jit(solution)/shard_map/dot_general | solution.py:35
  373.4 2.6 gather_fusion.3
  376.0 4.8 %all-to-all-start.2 = ((bf16[8,64,512]{2,1,0:T(8,128)(2,1)}), bf16[8,64,512]{2,1,0:T(8,128)(2,1)S(1)}, u32[]{:S(2)}, u32[]{:S(2)}) async-start(bf16[8,64,512]{2,1,0:T(8,128)(2,1)} %bitcast.11), calls=%async_computation.2 | async-start | bytes 1048576 | tf_op jit(solution)/shard_map/all_to_all | solution.py:69
  380.8 3.8 sort.32
  384.6 2.6 gather_fusion.2
  387.2 9.0 %all-to-all-done.2 = bf16[8,64,512]{2,1,0:T(8,128)(2,1)S(1)} async-done(((bf16[8,64,512]{2,1,0:T(8,128)(2,1)}), bf16[8,64,512]{2,1,0:T(8,128)(2,1)S(1)}, u32[]{:S(2)}, u32[]{:S(2)}) %all-to-all-start.2) | async-done | bytes 524320 | tf_op jit(solution)/shard_map/all_to_all | solution.py:69
  396.2 2.6 gather_fusion.4
  (37 shorter events, 5.5 us)
Async XLA Ops:
  7.2 348.3 %copy-start = (f32[4,128,64]{1,2,0:T(8,128)S(1)}, f32[4,128,64]{1,2,0:T(8,128)}, u32[]{:S(2)}) copy-start(f32[4,128,64]{1,2,0:T(8,128)} %param.8) | copy-start | bytes 393220
  7.2 109.1 %all-gather.4.cloned.1.call-start = ((), (), s32[]{:S(2)}) async-start(), calls=%async_computation.3 | async-start | bytes 12582912 | tf_op jit(solution)/shard_map/all_gather | solution.py:29
  7.9 192.1 %all-gather.6.cloned.1.call-start = ((), (), s32[]{:S(2)}) async-start(), calls=%async_computation.4 | async-start | bytes 9437184 | tf_op jit(solution)/shard_map/all_gather | solution.py:32
  8.7 203.2 %copy-start.1 = (s32[512]{0:T(512)S(1)}, s32[512]{0:T(512)}, u32[]{:S(2)}) copy-start(s32[512]{0:T(512)} %param.9) | copy-start | bytes 6148
  8.7 256.4 %all-reduce.2.cloned.1.call-start = ((), (), s32[]{:S(2)}) async-start(), calls=%async_computation.5 | async-start | bytes 524288 | tf_op jit(solution)/shard_map/psum | solution.py:14
  211.3 151.8 %all-gather.8.cloned.1.call-start = ((), (), s32[]{:S(2)}) async-start(), calls=%async_computation.6 | async-start | bytes 9437184 | tf_op jit(solution)/shard_map/all_gather | solution.py:37
  219.9 8.7 %all-to-all-start = ((s32[8,64,1]{1,2,0:T(1,128)}), s32[8,64,1]{1,2,0:T(1,128)S(1)}, u32[]{:S(2)}, u32[]{:S(2)}) async-start(s32[8,64,1]{1,2,0:T(1,128)} %bitcast.7), calls=%async_computation | async-start | bytes 8192 | tf_op jit(solution)/shard_map/all_to_all | solution.py:63
  359.5 16.6 %all-to-all-start.1 = ((bf16[8,64,256]{2,1,0:T(8,128)(2,1)}), bf16[8,64,256]{2,1,0:T(8,128)(2,1)S(1)}, u32[]{:S(2)}, u32[]{:S(2)}) async-start(bf16[8,64,256]{2,1,0:T(8,128)(2,1)} %bitcast.9), calls=%async_computation.1 | async-start | bytes 524288 | tf_op jit(solution)/shard_map/all_to_all | solution.py:66
  376.0 20.1 %all-to-all-start.2 = ((bf16[8,64,512]{2,1,0:T(8,128)(2,1)}), bf16[8,64,512]{2,1,0:T(8,128)(2,1)S(1)}, u32[]{:S(2)}, u32[]{:S(2)}) async-start(bf16[8,64,512]{2,1,0:T(8,128)(2,1)} %bitcast.11), calls=%async_computation.2 | async-start | bytes 1048576 | tf_op jit(solution)/shard_map/all_to_all | solution.py:69
Sparse Core Ops, SparseCore 0:
  9.6 106.6 all-gather.3
  117.9 82.0 all-gather.5
  211.4 53.5 all-reduce.1
  266.6 81.1 all-gather.7
where the time goes:
time: 406 us; the launch traced here: 405 us
  waiting for transfers between devices  242 us (60%)
  other arithmetic  98 us (24%)
  matrix products  23.4 us (6%)
  local copies, waits for them, and re-layouts  15.7 us (4%)
  between operations  13.9 us (3%)
  starting transfers between devices  12.1 us (3%)
    all_gather x1, waiting for transfers between devices, per_device(): gathered = lax.all_gather(hidden_states, 'head', axis=1, tiled=True)  108 us
    all_gather x1, waiting for transfers between devices, per_device(): lax.all_gather(key_projection_weight, ('seq', 'sub'), axis=0, tiled=True)  83.7 us
    another operation x4, other arithmetic, per_device(): factor = jnp.linalg.cholesky(regular)  47.1 us
    another operation x3, other arithmetic, per_device(): lax.linalg.triangular_solve(factor, by_head, left_side=False, lower=True,...  39.4 us
    psum x1, waiting for transfers between devices, covariance_sum(): summed = lax.psum(local_terms, ('seq', 'sub'))  34.9 us
    dot_general x1, matrix products, per_device(): jnp.dot(gathered, lax.all_gather(key_projection_weight, ('seq', 'sub'), a...  10.3 us
    dot_general x1, matrix products, per_device(): jnp.dot(gathered, lax.all_gather(value_projection_weight, ('seq', 'sub'),...  10.2 us
    all_to_all x1, waiting for transfers between devices, per_device(): lax.all_to_all(value_cache[local_rows], ('seq', 'sub'), split_axis=0, con...  9 us
  transfers between devices with their start and end apart: 7, of which 5 were waited for; matrix products, arithmetic and copies ran while one was open for 30% of the time, Pallas kernels for 0%

commit v1 on v0

--- a/solution.py
+++ b/solution.py
@@ -11,7 +11,8 @@
     local_terms = jnp.einsum(
         "thi,thj->hij", per_head_keys, per_head_keys, preferred_element_type=jnp.float32
     )
-    summed = lax.psum(local_terms, ("seq", "sub"))
+    partial = lax.psum(local_terms, "sub")
+    summed = lax.psum(partial, "seq")
     return summed / token_total
 
 

time: 406 us -> 470 us (1.16)
  waiting for transfers between devices: 242 us -> 308 us
    all_gather x1, waiting for transfers between devices: 0.02 us -> 83.2 us  [per_device(): lax.all_gather(value_projection_weight, ('seq', 'sub'), axis=0, tiled=True)]
    psum x1 -> x2, waiting for transfers between devices: 34.9 us -> 22.9 us  [the longest x1 22.9 us: covariance_sum(): summed = lax.psum(partial, 'seq')]
    all_to_all x1, waiting for transfers between devices: 9 us -> 0.01 us  [per_device(): lax.all_to_all(value_cache[local_rows], ('seq', 'sub'), split_axis=0, con...]
  transfers between devices with their start and end apart: 7 -> 8, of which waited for: 5 -> 6; matrix products, arithmetic and copies ran while one was open for 30% -> 26% of each run, Pallas kernels for 0% -> 0%
where the time goes in v1:
time: 470 us; the launch traced here: 469 us
  waiting for transfers between devices  308 us (66%)
  other arithmetic  98 us (21%)
  matrix products  23.4 us (5%)
  local copies, waits for them, and re-layouts  15.7 us (3%)
  between operations  14 us (3%)
  starting transfers between devices  10.6 us (2%)
    all_gather x1, waiting for transfers between devices, per_device(): gathered = lax.all_gather(hidden_states, 'head', axis=1, tiled=True)  108 us
    all_gather x1, waiting for transfers between devices, per_device(): lax.all_gather(key_projection_weight, ('seq', 'sub'), axis=0, tiled=True)  83.7 us
    all_gather x1, waiting for transfers between devices, per_device(): lax.all_gather(value_projection_weight, ('seq', 'sub'), axis=0, tiled=True)  83.2 us
    another operation x4, other arithmetic, per_device(): factor = jnp.linalg.cholesky(regular)  47.1 us
    another operation x3, other arithmetic, per_device(): lax.linalg.triangular_solve(factor, by_head, left_side=False, lower=True,...  39.4 us
    psum x1, waiting for transfers between devices, covariance_sum(): summed = lax.psum(partial, 'seq')  22.9 us
    dot_general x1, matrix products, per_device(): jnp.dot(gathered, lax.all_gather(key_projection_weight, ('seq', 'sub'), a...  10.3 us
    dot_general x1, matrix products, per_device(): jnp.dot(gathered, lax.all_gather(value_projection_weight, ('seq', 'sub'),...  10.2 us
  transfers between devices with their start and end apart: 8, of which 6 were waited for; matrix products, arithmetic and copies ran while one was open for 26% of the time, Pallas kernels for 0%

profile of v1, /device:TPU:0, one launch (start us, length us, event | category | flops | bytes accessed | tf_op | source)
XLA Modules:
  0.0 469.5 jit_solution(11247304850250110608)
XLA Ops:
  8.7 107.6 %all-gather.4.cloned.1.call-done = bf16[512,8192]{1,0:T(8,128)(2,1)} async-done(((bf16[512,4096]{1,0:T(8,128)(2,1)}), bf16[512,8192]{1,0:T(8,128)(2,1)}) %all-gather.4.cloned.1.call-update) | async-done | bytes 8388624 | tf_op jit(solution)/shard_map/all_gather | solution.py:30
  116.3 83.7 %all-gather.6.cloned.1.call-done = bf16[8192,512]{1,0:T(8,128)(2,1)} async-done(((bf16[1024,512]{1,0:T(8,128)(2,1)}), bf16[8192,512]{1,0:T(8,128)(2,1)}) %all-gather.6.cloned.1.call-update) | async-done | bytes 8388624 | tf_op jit(solution)/shard_map/all_gather | solution.py:33
  200.0 10.3 %convolution_convert_fusion.1 = bf16[512,512]{0,1:T(8,128)(2,1)S(1)} fusion(bf16[512,8192]{1,0:T(8,128)(2,1)} %all-gather.4.cloned.1.call-done, bf16[8192,512]{1,0:T(8,128)(2,1)} %all-gather.6.cloned.1.call-done), kind=kOutput, calls=%fused_computation.6 | convolution fusion | flops 4295229440 | bytes 17301504 | tf_op jit(solution)/shard_map/dot_general | solution.py:31
  211.9 3.8 sort.31
  215.7 3.5 gather_fusion
  219.9 3.3 all-to-all-start
  223.3 5.3 %all-to-all-done = s32[8,64,1]{1,2,0:T(1,128)S(1)} async-done(((s32[8,64,1]{1,2,0:T(1,128)}), s32[8,64,1]{1,2,0:T(1,128)S(1)}, u32[]{:S(2)}, u32[]{:S(2)}) %all-to-all-start) | async-done | bytes 2080 | tf_op jit(solution)/shard_map/all_to_all | solution.py:64
  230.0 83.2 %all-gather.8.cloned.1.call-done = bf16[8192,512]{1,0:T(8,128)(2,1)} async-done(((bf16[1024,512]{1,0:T(8,128)(2,1)}), bf16[8192,512]{1,0:T(8,128)(2,1)}) %all-gather.8.cloned.1.call-update) | async-done | bytes 8388624 | tf_op jit(solution)/shard_map/all_gather | solution.py:38
  313.2 10.2 %convolution_convert_fusion = bf16[512,512]{1,0:T(8,128)(2,1)S(1)} fusion(bf16[512,8192]{1,0:T(8,128)(2,1)} %all-gather.4.cloned.1.call-done, bf16[8192,512]{1,0:T(8,128)(2,1)} %all-gather.8.cloned.1.call-done), kind=kOutput, calls=%fused_computation.5 | convolution fusion | flops 4295229440 | bytes 17301504 | tf_op jit(solution)/shard_map/dot_general | solution.py:36
  323.7 2.6 gather_fusion.3
  326.3 3.7 all-to-all-start.2
  330.0 22.9 %all-reduce.5.cloned.1.call-done = f32[4,128,128]{2,1,0:T(8,128)} async-done(((f32[4,128,128]{2,1,0:T(8,128)}), f32[4,128,128]{2,1,0:T(8,128)}) %all-reduce.5.cloned.1.call-update) | async-done | bytes 262160 | tf_op jit(solution)/shard_map/psum | solution.py:15
  352.9 1.1 select_reduce_fusion.1
  354.0 1.0 multiply_add_fusion
  355.2 1.1 fusion.3
  356.2 46.9 %custom-call.7 = f32[4,128,128]{2,1,0:T(8,128)S(1)} custom-call(f32[4,128,128]{2,1,0:T(8,128)S(1)} %fusion.3), custom_call_target="Cholesky" | custom-call | tf_op jit(solution)/shard_map/jit(cholesky)/cholesky | solution.py:47
  403.4 39.3 %custom-call.8 = f32[4,1,128,128]{2,3,1,0:T(8,128)S(1)} custom-call(f32[4,1,128,128]{3,2,1,0:T(8,128)S(1)} %select_bitcast_fusion), custom_call_target="InvertDiagBlocksLowerTriangular" | custom-call | tf_op jit(solution)/shard_map/triangular_solve | solution.py:51
  443.3 1.3 convolution_convert_fusion.2
  444.7 2.6 gather_fusion.1
  447.3 3.4 all-to-all-start.1
  450.7 3.8 sort.32
  454.5 2.6 gather_fusion.4
  457.2 3.2 all-to-all-done.1
  460.4 2.6 gather_fusion.2
  (40 shorter events, 6.6 us)
Async XLA Ops:
  7.2 436.2 %copy-start = (f32[4,128,64]{1,2,0:T(8,128)S(1)}, f32[4,128,64]{1,2,0:T(8,128)}, u32[]{:S(2)}) copy-start(f32[4,128,64]{1,2,0:T(8,128)} %param.8) | copy-start | bytes 393220
  7.2 109.1 %all-gather.4.cloned.1.call-start = ((), (), s32[]{:S(2)}) async-start(), calls=%async_computation.3 | async-start | bytes 12582912 | tf_op jit(solution)/shard_map/all_gather | solution.py:30
  7.9 192.1 %all-gather.6.cloned.1.call-start = ((), (), s32[]{:S(2)}) async-start(), calls=%async_computation.4 | async-start | bytes 9437184 | tf_op jit(solution)/shard_map/all_gather | solution.py:33
  8.7 203.2 %copy-start.1 = (s32[512]{0:T(512)S(1)}, s32[512]{0:T(512)}, u32[]{:S(2)}) copy-start(s32[512]{0:T(512)} %param.9) | copy-start | bytes 6148
  8.7 221.3 %all-reduce.3.cloned.1.call-start = ((), (), s32[]{:S(2)}) async-start(), calls=%async_computation.5 | async-start | bytes 524288 | tf_op jit(solution)/shard_map/psum | solution.py:14
  211.3 101.8 %all-gather.8.cloned.1.call-start = ((), (), s32[]{:S(2)}) async-start(), calls=%async_computation.7 | async-start | bytes 9437184 | tf_op jit(solution)/shard_map/all_gather | solution.py:38
  219.9 8.7 %all-to-all-start = ((s32[8,64,1]{1,2,0:T(1,128)}), s32[8,64,1]{1,2,0:T(1,128)S(1)}, u32[]{:S(2)}, u32[]{:S(2)}) async-start(s32[8,64,1]{1,2,0:T(1,128)} %bitcast.7), calls=%async_computation | async-start | bytes 8192 | tf_op jit(solution)/shard_map/all_to_all | solution.py:64
  223.2 129.7 %all-reduce.5.cloned.1.call-start = ((), (), s32[]{:S(2)}) async-start(), calls=%async_computation.6 | async-start | bytes 524288 | tf_op jit(solution)/shard_map/psum | solution.py:15
  326.3 121.0 %all-to-all-start.2 = ((bf16[8,64,512]{2,1,0:T(8,128)(2,1)}), bf16[8,64,512]{2,1,0:T(8,128)(2,1)S(1)}, u32[]{:S(2)}, u32[]{:S(2)}) async-start(bf16[8,64,512]{2,1,0:T(8,128)(2,1)} %bitcast.11), calls=%async_computation.2 | async-start | bytes 1048576 | tf_op jit(solution)/shard_map/all_to_all | solution.py:70
  447.3 13.1 %all-to-all-start.1 = ((bf16[8,64,256]{2,1,0:T(8,128)(2,1)}), bf16[8,64,256]{2,1,0:T(8,128)(2,1)S(1)}, u32[]{:S(2)}, u32[]{:S(2)}) async-start(bf16[8,64,256]{2,1,0:T(8,128)(2,1)} %bitcast.9), calls=%async_computation.1 | async-start | bytes 524288 | tf_op jit(solution)/shard_map/all_to_all | solution.py:67
Sparse Core Ops, SparseCore 0:
  9.6 106.6 all-gather.3
  117.9 82.0 all-gather.5
  211.4 16.8 all-reduce.2
  229.9 83.2 all-gather.7
  315.5 37.4 all-reduce.4
